TPU v7x, 512 devices: a whole 4x4x16 slice. The times are simulated.
512 devices in a mesh: dp: 16 (over z), mp: 32 (over y, x, core).
Axes of the slice: x: 4, y: 4, z: 16, core: 2. Of those that a mesh axis runs over, the one named last changes fastest.
Arguments:
- output_gradient: bfloat16 [12288, 8192], P('dp', 'mp'), may hold values from -6 to 6
- saved_gate_value: bfloat16 [12288, 14336], P('dp', 'mp'), may hold values from -6 to 6
- saved_up_value: bfloat16 [12288, 14336], P('dp', 'mp'), may hold values from -6 to 6
- down_weight: bfloat16 [14336, 8192], P('mp', 'dp'), may hold values from -0.046875 to 0.046875
- adapter_first_weight: bfloat16 [64, 64, 14336], P('dp', None, 'mp'), may hold values from -0.046875 to 0.046875
- adapter_second_weight: bfloat16 [64, 64, 8192], P('dp', None, 'mp'), may hold values from -0.0625 to 0.0625
- adapter_of_block: int32 [192], replicated, may hold values from 0 to 63, as said below
- slot_of_adapter: int32 [64], replicated, may hold values from 0 to 63, as said below
Outputs:
- d_gate: bfloat16 [12288, 14336], P('dp', 'mp')
- d_up: bfloat16 [12288, 14336], P('dp', 'mp')
- grad_a: float32 [64, 64, 14336], P('dp', None, 'mp')
- grad_b: float32 [64, 64, 8192], P('dp', None, 'mp')
Inputs may be any that keep to these rules, and one draw needn't show every extreme that they name: `adapter_of_block`: block k holds tokens k * 64 to k * 64 + 63; group g holds blocks g * 12 onward. Slot s belongs to owner s // 4; the blocks of one group use adapters of any one owner at most 1 times, and in every draw one owner takes exactly 1 block of every group. A permutation: adapter a is stored at index slot_of_adapter[a] of adapter_first_weight, adapter_second_weight, grad_a and grad_b.
All inputs are finite; a program needn't handle non-finite values.
Results may differ from a plain program's by a relative error of at most 0.0057.
Values may be sent and summed in bfloat16 or wider, within the bound.
A program may use at most 128 MiB of HBM per device.

v0:
```python
import jax
import jax.numpy as jnp
from jax import lax
from jax.sharding import PartitionSpec as P

ADAPTER_RANK = 64
BLK = 64


adapter_scale = 2.0


def in_one_piece(arrays, axis, split_dim, concat_dim, along):
    both = jnp.concatenate(arrays, axis=along)
    filled, at, outs = (
        lax.all_to_all(both, axis, split_axis=split_dim, concat_axis=concat_dim, tiled=True),
        0,
        [],
    )
    for a in arrays:
        outs.append(lax.slice_in_dim(filled, at, at + a.shape[along], axis=along))
        at += a.shape[along]
    return tuple(outs)


def shards(
    output_gradient,
    saved_gate_value,
    saved_up_value,
    down_weight,
    adapter_first_weight,
    adapter_second_weight,
    adapter_of_block,
    slot_of_adapter,
):
    groups = lax.axis_size("dp")
    my_group = lax.axis_index("dp")
    tok_rows = output_gradient.shape[0]
    blocks = tok_rows // BLK
    owner_totals = adapter_first_weight.shape[0]
    adapters = slot_of_adapter.shape[0]
    ff_local = saved_gate_value.shape[1]
    d_local = output_gradient.shape[1]
    capacity = (blocks + groups - 1) // groups
    gate_float = saved_gate_value.astype(jnp.float32)
    up_float = saved_up_value.astype(jnp.float32)
    squash = jax.nn.sigmoid(gate_float)
    activated = gate_float * squash
    hidden = (activated * up_float).astype(jnp.bfloat16)
    match_table = adapter_of_block[:, None] == jnp.arange(adapters, dtype=jnp.int32)[None, :]
    slot_of_block = jnp.sum(jnp.where(match_table, slot_of_adapter[None, :], 0), axis=1)
    owners = (slot_of_block // owner_totals).reshape(groups, blocks)
    local_slot = (slot_of_block % owner_totals).reshape(groups, blocks)
    block_index = jnp.arange(blocks, dtype=jnp.int32)
    earlier = (owners[:, :, None] == owners[:, None, :]) & (
        block_index[None, None, :] < block_index[None, :, None]
    )
    ranks = jnp.sum(earlier.astype(jnp.int32), axis=2)
    owned_here = owners == my_group
    rank_values = jnp.arange(capacity, dtype=jnp.int32)
    hits = owned_here[:, None, :] & (ranks[:, None, :] == rank_values[None, :, None])
    incoming_valid = jnp.any(hits, axis=2)
    arriving_slot = jnp.sum(jnp.where(hits, local_slot[:, None, :], 0), axis=2)
    own_owner = lax.dynamic_index_in_dim(owners, my_group, 0, keepdims=False)
    own_rank = lax.dynamic_index_in_dim(ranks, my_group, 0, keepdims=False)
    own_index = own_owner * capacity + own_rank
    a_send = jnp.where(
        incoming_valid[:, :, None, None],
        jnp.take(adapter_first_weight, arriving_slot, axis=0),
        jnp.zeros((), adapter_first_weight.dtype),
    )
    b_send = jnp.where(
        incoming_valid[:, :, None, None],
        jnp.take(adapter_second_weight, arriving_slot, axis=0),
        jnp.zeros((), adapter_second_weight.dtype),
    )
    a_recv, b_recv = in_one_piece((a_send, b_send), "dp", 0, 0, 3)
    first_factor_blocks = jnp.take(
        a_recv.reshape(groups * capacity, ADAPTER_RANK, ff_local), own_index, axis=0
    )
    second_factor_blocks = jnp.take(
        b_recv.reshape(groups * capacity, ADAPTER_RANK, d_local), own_index, axis=0
    )
    hidden_blocks = hidden.reshape(blocks, BLK, ff_local)
    output_blocks = output_gradient.reshape(blocks, BLK, d_local)
    down_part = jnp.einsum(
        "btf,brf->btr", hidden_blocks, first_factor_blocks, preferred_element_type=jnp.float32
    )
    back_part = jnp.einsum(
        "btd,brd->btr", output_blocks, second_factor_blocks, preferred_element_type=jnp.float32
    )
    summed_total = lax.psum(jnp.concatenate([down_part, back_part], axis=2), "mp")
    downward_factor = summed_total[:, :, :ADAPTER_RANK].astype(jnp.bfloat16)
    backward_factor = (adapter_scale * summed_total[:, :, ADAPTER_RANK:]).astype(jnp.bfloat16)
    out_whole = lax.all_gather(output_gradient, "mp", axis=1, tiled=True)
    side_term = jnp.einsum(
        "btr,brf->btf", backward_factor, first_factor_blocks, preferred_element_type=jnp.float32
    ).reshape(tok_rows, ff_local)
    d_hidden = side_term + lax.dot_general(
        out_whole,
        lax.all_gather(down_weight, "dp", axis=1, tiled=True),
        (((1,), (1,)), ((), ())),
        preferred_element_type=jnp.float32,
    )
    d_gate = (d_hidden * up_float * squash * (1.0 + gate_float * (1.0 - squash))).astype(
        jnp.bfloat16
    )
    d_up = (d_hidden * activated).astype(jnp.bfloat16)
    group_values = jnp.arange(groups, dtype=jnp.int32)
    route_table = (own_owner[None, None, :] == group_values[:, None, None]) & (
        own_rank[None, None, :] == rank_values[None, :, None]
    )
    route_valid = jnp.any(route_table, axis=2)
    route_block = jnp.sum(jnp.where(route_table, block_index[None, None, :], 0), axis=2)
    factors = jnp.concatenate([downward_factor, backward_factor], axis=2)
    send_h = jnp.where(
        route_valid[:, :, None, None],
        jnp.take(hidden_blocks, route_block, axis=0),
        jnp.zeros((), jnp.bfloat16),
    )
    send_o = jnp.where(
        route_valid[:, :, None, None],
        jnp.take(output_blocks, route_block, axis=0),
        jnp.zeros((), jnp.bfloat16),
    )
    send_f = jnp.where(
        route_valid[:, :, None, None],
        jnp.take(factors, route_block, axis=0),
        jnp.zeros((), jnp.bfloat16),
    )
    recv_h, recv_o, recv_f = (
        lax.all_to_all(send_h, "dp", split_axis=0, concat_axis=0, tiled=True),
        lax.all_to_all(send_o, "dp", split_axis=0, concat_axis=0, tiled=True),
        lax.all_to_all(send_f, "dp", split_axis=0, concat_axis=0, tiled=True),
    )
    terms_a = jnp.einsum(
        "gctr,gctf->gcrf",
        recv_f[:, :, :, ADAPTER_RANK:],
        recv_h,
        preferred_element_type=jnp.float32,
    ).astype(jnp.bfloat16)
    terms_b = (
        adapter_scale
        * jnp.einsum(
            "gctr,gctd->gcrd",
            recv_f[:, :, :, :ADAPTER_RANK],
            recv_o,
            preferred_element_type=jnp.float32,
        )
    ).astype(jnp.bfloat16)
    flat_slot = arriving_slot.reshape(groups * capacity)
    flat_valid = incoming_valid.reshape(groups * capacity)
    selector = (
        (flat_slot[None, :] == jnp.arange(owner_totals, dtype=jnp.int32)[:, None])
        & flat_valid[None, :]
    ).astype(jnp.bfloat16)
    grad_a = jnp.dot(
        selector,
        terms_a.reshape(groups * capacity, ADAPTER_RANK * ff_local),
        preferred_element_type=jnp.float32,
    ).reshape(owner_totals, ADAPTER_RANK, ff_local)
    grad_b = jnp.dot(
        selector,
        terms_b.reshape(groups * capacity, ADAPTER_RANK * d_local),
        preferred_element_type=jnp.float32,
    ).reshape(owner_totals, ADAPTER_RANK, d_local)
    return (d_gate, d_up, grad_a, grad_b)


def solution(mesh):
    in_specs = (
        P("dp", "mp"),
        P("dp", "mp"),
        P("dp", "mp"),
        P("mp", "dp"),
        P("dp", None, "mp"),
        P("dp", None, "mp"),
        P(),
        P(),
    )
    out_specs = (P("dp", "mp"), P("dp", "mp"), P("dp", None, "mp"), P("dp", None, "mp"))
    return jax.shard_map(shards, mesh=mesh, in_specs=in_specs, out_specs=out_specs, check_vma=False)
```

profile of v0, /device:TPU:1, one launch (start us, length us, event | category | flops | bytes accessed | tf_op | source)
XLA Modules:
  0.0 352.2 jit_solution(18268147364254262424)
XLA Ops:
  8.0 0.0 copy-start
  8.0 0.8 select_reduce_fusion
  8.9 0.1 reduce_sum.45
  9.0 0.1 reduce_sum.47
  9.0 0.1 copy.56
  9.1 0.1 copy.60
  9.2 0.4 convert_reduce_fusion
  9.6 0.2 dynamic-slice_reduce_fusion
  9.8 0.1 select_reduce_fusion.1
  9.9 0.1 copy.61
  10.1 0.6 gather_fusion
  10.7 0.0 copy-done.4
  10.8 0.6 gather_fusion.1
  11.3 0.2 fusion.12
  11.6 0.1 fusion.21
  11.7 1.6 maximum_bitcast_fusion
  13.4 15.9 %all-to-all-start = ((bf16[16,1,64,704]{3,2,1,0:T(8,128)(2,1)}), bf16[16,1,64,704]{3,2,1,0:T(8,128)(2,1)S(1)}, u32[]{:S(2)}, u32[]{:S(2)}) async-start(bf16[16,1,64,704]{3,2,1,0:T(8,128)(2,1)} %maximum_bitcast_fusion), calls=%async_computation | async-start | bytes 3145728 | tf_op jit(solution)/shard_map/all_to_all | solution.py:16
  29.2 0.0 all-reduce.2.cloned.1.call-start
  29.3 1.5 fusion
  30.8 0.3 copy.55
  31.1 67.1 %all-to-all-done = bf16[16,1,64,704]{3,2,1,0:T(8,128)(2,1)S(1)} async-done(((bf16[16,1,64,704]{3,2,1,0:T(8,128)(2,1)}), bf16[16,1,64,704]{3,2,1,0:T(8,128)(2,1)S(1)}, u32[]{:S(2)}, u32[]{:S(2)}) %all-to-all-start) | async-done | bytes 1441824 | tf_op jit(solution)/shard_map/all_to_all | solution.py:16
  98.2 1.1 slice_bitcast_fusion
  99.3 1.8 gather_fusion.2
  101.2 1.0 slice_bitcast_fusion.1
  102.2 1.7 gather_fusion.3
  103.9 0.4 fusion.26
  104.3 0.0 copy-done.3
  104.3 0.3 convolution_bitcast_fusion
  104.7 0.9 pad_maximum_fusion
  105.6 0.0 all-reduce.2.cloned.1.call-update
  105.6 0.0 all-gather.5.cloned.1.call-start
  105.7 0.5 all-gather.5.cloned.1.call-update
  106.2 0.0 all-gather.3.cloned.1.call-start
  106.2 0.5 all-gather.3.cloned.1.call-update
  106.8 0.6 gather_fusion.5
  107.4 0.1 fusion.37
  107.5 1.2 fusion.11
  108.7 11.5 %all-to-all-start.2 = ((bf16[16,1,64,448]{3,2,1,0:T(8,128)(2,1)}), bf16[16,1,64,448]{3,2,1,0:T(8,128)(2,1)S(1)}, u32[]{:S(2)}, u32[]{:S(2)}) async-start(bf16[16,1,64,448]{3,2,1,0:T(8,128)(2,1)} %fusion.11), calls=%async_computation.2 | async-start | bytes 2097152 | tf_op jit(solution)/shard_map/all_to_all | solution.py:132
  120.2 122.6 %all-reduce.2.cloned.1.call-done = f32[12,64,128]{2,1,0:T(8,128)} async-done(((f32[12,64,128]{2,1,0:T(8,128)}), f32[12,64,128]{2,1,0:T(8,128)}) %all-reduce.2.cloned.1.call-update) | async-done | bytes 393232 | tf_op jit(solution)/shard_map/psum | solution.py:92
  242.8 1.0 slice.55
  243.8 0.0 copy-start.2
  243.8 1.2 fusion.22
  245.1 0.1 pad_maximum_fusion.1
  245.2 0.6 gather_fusion.4
  245.8 0.8 fusion.28
  246.6 0.0 all-to-all-done.2
  246.6 12.0 %all-to-all-start.1 = ((bf16[16,1,64,128]{3,2,1,0:T(8,128)(2,1)}), bf16[16,1,64,128]{3,2,1,0:T(8,128)(2,1)S(1)}, u32[]{:S(2)}, u32[]{:S(2)}) async-start(bf16[16,1,64,128]{3,2,1,0:T(8,128)(2,1)} %fusion.28), calls=%async_computation.1 | async-start | bytes 524288 | tf_op jit(solution)/shard_map/all_to_all | solution.py:134
  258.6 0.6 gather_fusion.6
  259.2 0.9 fusion.20
  260.2 12.5 %all-to-all-done.1 = bf16[16,1,64,128]{3,2,1,0:T(8,128)(2,1)S(1)} async-done(((bf16[16,1,64,128]{3,2,1,0:T(8,128)(2,1)}), bf16[16,1,64,128]{3,2,1,0:T(8,128)(2,1)S(1)}, u32[]{:S(2)}, u32[]{:S(2)}) %all-to-all-start.1) | async-done | bytes 262176 | tf_op jit(solution)/shard_map/all_to_all | solution.py:134
  272.6 10.3 %all-to-all-start.3 = ((bf16[16,1,64,256]{3,2,1,0:T(8,128)(2,1)}), bf16[16,1,64,256]{3,2,1,0:T(8,128)(2,1)}, u32[]{:S(2)}, u32[]{:S(2)}) async-start(bf16[16,1,64,256]{3,2,1,0:T(8,128)(2,1)} %fusion.20), calls=%async_computation.3 | async-start | bytes 1048576 | tf_op jit(solution)/shard_map/all_to_all | solution.py:133
  282.9 1.5 fusion.25
  284.5 1.5 copy.66
  286.0 0.7 convolution_convert_fusion
  286.7 1.2 reshape.572
  287.9 1.2 dot_general.41
  289.1 0.7 fusion.13
  289.8 1.0 copy.74
  290.8 15.1 %all-to-all-done.3 = bf16[16,1,64,256]{3,2,1,0:T(8,128)(2,1)} async-done(((bf16[16,1,64,256]{3,2,1,0:T(8,128)(2,1)}), bf16[16,1,64,256]{3,2,1,0:T(8,128)(2,1)}, u32[]{:S(2)}, u32[]{:S(2)}) %all-to-all-start.3) | async-done | bytes 524320 | tf_op jit(solution)/shard_map/all_to_all | solution.py:133
  305.9 1.5 fusion.8
  307.5 0.4 fusion.15
  307.9 0.8 copy.75
  308.6 21.2 %all-gather.3.cloned.1.call-done = bf16[768,8192]{1,0:T(8,128)(2,1)} async-done(((bf16[768,256]{1,0:T(8,128)(2,1)}), bf16[768,8192]{1,0:T(8,128)(2,1)}) %all-gather.3.cloned.1.call-update) | async-done | bytes 12582928 | tf_op jit(solution)/shard_map/all_gather | solution.py:95
  329.9 14.9 %multiply_convert_fusion = (bf16[768,448]{0,1:T(8,128)(2,1)}, bf16[768,448]{0,1:T(8,128)(2,1)}) fusion(bf16[768,448]{0,1:T(8,128)(2,1)S(1)} %copy-done.7, bf16[768,448]{0,1:T(8,128)(2,1)} %param.10, f32[768,448]{0,1:T(8,128)S(1)} %copy-done.5, bf16[768,8192]{1,0:T(8,128)(2,1)} %all-gather.3.cloned.1.call-done, ...), kind=kOutput, calls=%fused_computation.23 | convolution fusion | flops 5642649600 | bytes 24051712 | tf_op jit(solution)/shard_map/dot_general | solution.py:99
  (25 shorter events, 0.2 us)
Async XLA Ops:
  8.0 2.1 copy-start
  8.0 2.7 copy-start.4
  13.3 15.9 %copy-start.6 = (bf16[768,448]{0,1:T(8,128)(2,1)S(1)}, bf16[768,448]{0,1:T(8,128)(2,1)}, u32[]{:S(2)}) copy-start(bf16[768,448]{0,1:T(8,128)(2,1)} %param.9) | copy-start | bytes 2064388
  13.4 84.9 %all-to-all-start = ((bf16[16,1,64,704]{3,2,1,0:T(8,128)(2,1)}), bf16[16,1,64,704]{3,2,1,0:T(8,128)(2,1)S(1)}, u32[]{:S(2)}, u32[]{:S(2)}) async-start(bf16[16,1,64,704]{3,2,1,0:T(8,128)(2,1)} %maximum_bitcast_fusion), calls=%async_computation | async-start | bytes 3145728 | tf_op jit(solution)/shard_map/all_to_all | solution.py:16
  29.2 213.6 %all-reduce.2.cloned.1.call-start = ((), (), s32[]{:S(2)}) async-start(), calls=%async_computation.4 | async-start | bytes 786432 | tf_op jit(solution)/shard_map/psum | solution.py:92
  101.1 3.2 copy-start.3
  102.2 2.1 copy-start.1
  105.6 203.0 %all-gather.5.cloned.1.call-start = ((), (), s32[]{:S(2)}) async-start(), calls=%async_computation.6 | async-start | bytes 7798784 | tf_op jit(solution)/shard_map/all_gather | solution.py:101
  106.2 223.7 %all-gather.3.cloned.1.call-start = ((), (), s32[]{:S(2)}) async-start(), calls=%async_computation.5 | async-start | bytes 12976128 | tf_op jit(solution)/shard_map/all_gather | solution.py:95
  108.7 137.9 %all-to-all-start.2 = ((bf16[16,1,64,448]{3,2,1,0:T(8,128)(2,1)}), bf16[16,1,64,448]{3,2,1,0:T(8,128)(2,1)S(1)}, u32[]{:S(2)}, u32[]{:S(2)}) async-start(bf16[16,1,64,448]{3,2,1,0:T(8,128)(2,1)} %fusion.11), calls=%async_computation.2 | async-start | bytes 2097152 | tf_op jit(solution)/shard_map/all_to_all | solution.py:132
  243.8 14.8 %copy-start.2 = (bf16[768,256]{1,0:T(8,128)(2,1)S(1)}, bf16[768,256]{1,0:T(8,128)(2,1)}, u32[]{:S(2)}) copy-start(bf16[768,256]{1,0:T(8,128)(2,1)} %param.8) | copy-start | bytes 1179652
  246.6 26.0 %all-to-all-start.1 = ((bf16[16,1,64,128]{3,2,1,0:T(8,128)(2,1)}), bf16[16,1,64,128]{3,2,1,0:T(8,128)(2,1)S(1)}, u32[]{:S(2)}, u32[]{:S(2)}) async-start(bf16[16,1,64,128]{3,2,1,0:T(8,128)(2,1)} %fusion.28), calls=%async_computation.1 | async-start | bytes 524288 | tf_op jit(solution)/shard_map/all_to_all | solution.py:134
  272.6 33.3 %all-to-all-start.3 = ((bf16[16,1,64,256]{3,2,1,0:T(8,128)(2,1)}), bf16[16,1,64,256]{3,2,1,0:T(8,128)(2,1)}, u32[]{:S(2)}, u32[]{:S(2)}) async-start(bf16[16,1,64,256]{3,2,1,0:T(8,128)(2,1)} %fusion.20), calls=%async_computation.3 | async-start | bytes 1048576 | tf_op jit(solution)/shard_map/all_to_all | solution.py:133
  290.8 39.1 %copy-start.5 = (f32[768,448]{0,1:T(8,128)S(1)}, f32[768,448]{0,1:T(8,128)}, u32[]{:S(2)}) copy-start(f32[768,448]{0,1:T(8,128)} %copy.66) | copy-start | bytes 4128772
  290.8 39.1 %copy-start.7 = (bf16[768,448]{0,1:T(8,128)(2,1)S(1)}, bf16[768,448]{0,1:T(8,128)(2,1)}, u32[]{:S(2)}) copy-start(bf16[768,448]{0,1:T(8,128)(2,1)} %param.9) | copy-start | bytes 2064388
Sparse Core Ops, SparseCore 0:
  105.7 137.0 all-reduce.1
Sparse Core Ops, SparseCore 1:
  108.2 135.6 all-gather.4
  246.7 83.1 all-gather.2
where the time goes:
time: 353 us; the launch traced here: 352 us
  waiting for transfers between devices  240 us (68%)
  starting transfers between devices  49.8 us (14%)
  matrix products  20.5 us (6%)
  local copies, waits for them, and re-layouts  16 us (5%)
  between operations  15.8 us (4%)
  other arithmetic  10.5 us (3%)
    psum x1, waiting for transfers between devices, shards(): lax.psum(jnp.concatenate([down_part, back_part], axis=2), 'mp')  123 us
    all_to_all x1, waiting for transfers between devices, in_one_piece(): lax.all_to_all(both, axis, split_axis=split_dim, concat_axis=concat_dim,...  67.1 us
    all_gather x1, waiting for transfers between devices, shards(): out_whole = lax.all_gather(output_gradient, 'mp', axis=1, tiled=True)  21.2 us
    all_to_all x1, starting transfers between devices, in_one_piece(): lax.all_to_all(both, axis, split_axis=split_dim, concat_axis=concat_dim,...  15.9 us
    all_to_all x1, waiting for transfers between devices, shards(): lax.all_to_all(send_o, 'dp', split_axis=0, concat_axis=0, tiled=True)  15.1 us
    dot_general x1, matrix products, shards(): lax.dot_general(out_whole, lax.all_gather(down_weight, 'dp', axis=1, tile...  14.9 us
    all_to_all x1, waiting for transfers between devices, shards(): lax.all_to_all(send_f, 'dp', split_axis=0, concat_axis=0, tiled=True)  12.5 us
    all_to_all x1, starting transfers between devices, shards(): lax.all_to_all(send_f, 'dp', split_axis=0, concat_axis=0, tiled=True)  12 us
  transfers between devices with their start and end apart: 7, of which 5 were waited for; matrix products, arithmetic and copies ran while one was open for 6% of the time, Pallas kernels for 0%

commit v1 on v0

v1 whole, which is shorter than its diff:
```python
import functools
import math

import jax
import jax.numpy as jnp
from jax import lax
from jax.experimental import pallas as pl
from jax.experimental.pallas import tpu as pltpu
from jax.sharding import PartitionSpec as P

BLK = 64
RANK = 64
MESH = pl.DeviceIdType.MESH
F32 = jnp.float32
BF16 = jnp.bfloat16


def dot(x, y, cx, cy):
    return lax.dot_general(x, y, (((cx,), (cy,)), ((), ())), preferred_element_type=F32)


def each(lo, hi, body):
    def step(i, carry):
        body(i)
        return carry

    lax.fori_loop(lo, hi, step, 0)


def tail_pack(x):
    return jnp.concatenate([x[:32], x[32:]], axis=1)


def tail_unpack(x):
    return jnp.concatenate([x[:, :64], x[:, 64:]], axis=0)


def kernel(
    nz, mp,
    blk_of, slot_in, slot_of, owner_of, hit_of, mask_in, og, og3, gate, up, w, a, b,
    dg, du, ga, gb,
    ogb, wb, ab, hs, hr, part, rsb, fac, bs, bb, acc, f1, f2,
    og_s, og_r, w_s, w_r, a_s, a_r, x_s, x_r, rs_s, rs_r, fg_s, fg_r, bk_s, bk_r, loc,
):
    xs = math.isqrt(mp // 2)
    ys = mp // 2 // xs
    rows, d_loc = og.shape
    nblk, _, ff = gate.shape
    own = a.shape[0]
    full = ff // 128
    half_rows = rows // 2
    g = lax.axis_index("dp")
    m = lax.axis_index("mp")

    def ring_to_mp(q):
        p, c = lax.div(q, 2), lax.rem(q, 2)
        y = lax.div(p, xs)
        x = lax.rem(lax.rem(p, xs) + ys * xs - y, xs)
        return (y * xs + x) * 2 + c

    chip = lax.div(m, 2)
    row = lax.div(chip, xs)
    q = (xs * row + lax.rem(lax.rem(chip, xs) + row, xs)) * 2 + lax.rem(m, 2)

    bar = pltpu.get_barrier_semaphore()

    def greet_z(d):
        pl.semaphore_signal(bar, inc=1, device_id=(lax.rem(g + d, nz), m), device_id_type=MESH)

    def greet_p(d):
        pl.semaphore_signal(bar, inc=1, device_id=(g, lax.rem(m + d, mp)), device_id_type=MESH)

    each(1, nz, greet_z)
    each(1, mp, greet_p)
    pl.semaphore_wait(bar, nz + mp - 2)

    class Ring:
        def __init__(self, n, pos, peer, first, buf, ssem, rsem):
            self.n, self.pos, self.peer, self.first, self.buf = n, pos, peer, first, buf
            self.ssem, self.rsem, self.size = ssem, rsem, n // 2

        def steps(self, d, h):
            return self.size if d == h else self.size - 1

        def at(self, d, s):
            return lax.rem(self.pos + (self.n - s if d == 0 else s), self.n)

        def copy(self, d, h, s, src=None):
            dst = self.buf(self.at(d, s), h)
            return pltpu.make_async_remote_copy(
                src_ref=dst if src is None else src,
                dst_ref=dst,
                send_sem=self.ssem.at[d, h, s],
                recv_sem=self.rsem.at[d, h, s],
                device_id=self.peer(lax.rem(self.pos + (1 if d == 0 else self.n - 1), self.n)),
                device_id_type=MESH,
            )

        def begin(self):
            for h in (0, 1):
                for d in (0, 1):
                    if self.steps(d, h) > 0:
                        self.copy(d, h, 0, self.first(h)).start()

        def arrived(self, d, h, s):
            ref = self.buf(self.at(d, s + 1), h)
            pltpu.make_async_remote_copy(
                src_ref=ref,
                dst_ref=ref,
                send_sem=self.ssem.at[d, h, s],
                recv_sem=self.rsem.at[d, h, s],
                device_id=self.peer(self.pos),
                device_id_type=MESH,
            ).wait_recv()

        def relay(self, s, last):
            for h in (0, 1):
                for d in (0, 1):
                    self.arrived(d, h, s - 1)
                    if d == h or not last:
                        self.copy(d, h, s).start()

        def finish(self):
            for d in (0, 1):
                self.arrived(d, d, self.size - 1)

        def sent(self):
            for h in (0, 1):
                for d in (0, 1):
                    each(0, self.steps(d, h), lambda s, d=d, h=h: self.copy(d, h, s).wait_send())

    plane = Ring(
        mp, q, lambda r: (g, ring_to_mp(r)),
        lambda h: og.at[pl.ds(h * half_rows, half_rows), :],
        lambda r, h: ogb.at[ring_to_mp(r), pl.ds(h * half_rows, half_rows), :],
        og_s, og_r,
    )
    wring = Ring(
        nz, g, lambda r: (r, m),
        lambda h: w.at[:, pl.ds(h * d_loc, d_loc)],
        lambda r, h: wb.at[r, h],
        w_s, w_r,
    )

    def some_a(r, h):
        return ab.at[pl.ds(r * own + h * (own // 2), own // 2)]

    aring = Ring(nz, g, lambda r: (r, m), lambda h: some_a(g, h), some_a, a_s, a_r)

    plane.begin()
    wring.begin()
    own_og = pltpu.make_async_copy(og, ogb.at[m], loc.at[0])
    own_og.start()

    for l in range(own):
        x = a[l].astype(F32)
        for k in range(full):
            ab[g * own + l, k * 64 : (k + 1) * 64, :] = a[l, :, k * 128 : (k + 1) * 128]
        ab[g * own + l, full * 64 :, :] = tail_pack(x[:, full * 128 :]).astype(BF16)

    def fill(o):
        at, hit = blk_of[o], hit_of[o]
        gf = gate[at].astype(F32)
        h = gf * jax.nn.sigmoid(gf) * up[at].astype(F32) * hit
        for k in range(full):
            hs[o, k * 64 : (k + 1) * 64, :] = h[:, k * 128 : (k + 1) * 128].astype(BF16)
        hs[o, full * 64 : full * 64 + 32, :] = tail_pack(h[:, full * 128 :]).astype(BF16)
        x = (og3[at].astype(F32) * hit).astype(BF16)
        for k in range(d_loc // 128):
            base = full * 64 + 32 + k * 64
            hs[o, base : base + 64, :] = x[:, k * 128 : (k + 1) * 128]

    each(0, nz, fill)
    aring.begin()

    def cross(src, dst, ssem, rsem, d):
        to = lax.rem(g + d, nz)
        return pltpu.make_async_remote_copy(
            src_ref=src.at[to], dst_ref=dst.at[g], send_sem=ssem.at[d], recv_sem=rsem.at[d],
            device_id=(to, m), device_id_type=MESH,
        )

    def crossed(dst, ssem, rsem, d):
        ref = dst.at[lax.rem(g + nz - d, nz)]
        pltpu.make_async_remote_copy(
            src_ref=ref, dst_ref=ref, send_sem=ssem.at[d], recv_sem=rsem.at[d],
            device_id=(g, m), device_id_type=MESH,
        ).wait_recv()

    each(1, nz, lambda d: cross(hs, hr, x_s, x_r, d).start())
    own_hs = pltpu.make_async_copy(hs.at[g], hr.at[g], loc.at[1])
    own_hs.start()

    acc[...] = jnp.zeros_like(acc)

    each(1, plane.size - 1, lambda s: plane.relay(s, False))
    plane.relay(plane.size - 1, True)

    plane.finish()
    own_og.wait()

    def hidden_of(j):
        parts = [hr[j, k * 64 : (k + 1) * 64, :] for k in range(full)]
        t = tail_unpack(hr[j, full * 64 : full * 64 + 32, :].astype(F32)).astype(BF16)
        return jnp.concatenate(parts + [t], axis=1)

    def grad_of(j):
        base = full * 64 + 32
        return jnp.concatenate(
            [hr[j, base + k * 64 : base + (k + 1) * 64, :] for k in range(d_loc // 128)], axis=1
        )

    def flat(src, dst, own_src, ssem, rsem, d):
        to = lax.rem(m + d, mp)
        return pltpu.make_async_remote_copy(
            src_ref=src.at[m if own_src else to], dst_ref=dst.at[m],
            send_sem=ssem.at[d], recv_sem=rsem.at[d], device_id=(g, to), device_id_type=MESH,
        )

    def flat_arrived(dst, ssem, rsem, d):
        ref = dst.at[lax.rem(m + mp - d, mp)]
        pltpu.make_async_remote_copy(
            src_ref=ref, dst_ref=ref, send_sem=ssem.at[d], recv_sem=rsem.at[d],
            device_id=(g, m), device_id_type=MESH,
        ).wait_recv()

    def stage_partial():
        own_hs.wait()
        each(1, nz, lambda d: crossed(hr, x_s, x_r, d))

        def one(j):
            idx = slot_in[j]
            down = dot(hidden_of(j), a[idx], 1, 1)
            back = dot(grad_of(j), b[idx], 1, 1)
            both = jnp.concatenate([down, back], axis=1)
            part[2 * j] = both[:32]
            part[2 * j + 1] = both[32:]

        each(0, nz, one)
        each(1, mp, lambda d: flat(part, rsb, False, rs_s, rs_r, d).start())

    lane = lax.broadcasted_iota(jnp.int32, (32, 128), 1)

    def stage_sum():
        rsb[m] = part[m]
        each(1, mp, lambda d: flat_arrived(rsb, rs_s, rs_r, d))
        total = lax.fori_loop(0, mp, lambda c, t: t + rsb[c], jnp.zeros((32, 128), F32))
        fac[m] = jnp.where(lane < 64, total, 2.0 * total).astype(BF16)
        each(1, mp, lambda d: flat(fac, fac, True, fg_s, fg_r, d).start())

    def stage_back():
        each(1, mp, lambda d: flat_arrived(fac, fg_s, fg_r, d))

        def one(j):
            top = pltpu.roll(fac[2 * j].astype(F32), 64, 1)
            bs[j] = jnp.where(lane < 64, top, fac[2 * j + 1].astype(F32)).astype(BF16)

        each(0, nz, one)
        bb[g] = bs[g]
        each(1, nz, lambda d: cross(bs, bb, bk_s, bk_r, d).start())

    def stage_grads():
        ga[...] = jnp.zeros_like(ga)
        gb[...] = jnp.zeros_like(gb)

        def one(j):
            f = jnp.concatenate([fac[2 * j], fac[2 * j + 1]], axis=0)
            pa = dot(f, hidden_of(j), 0, 0)[64:].astype(BF16).astype(F32)
            pb = (2.0 * dot(f, grad_of(j), 0, 0)[:64]).astype(BF16).astype(F32)
            for l in range(own):
                ga[l] += pa * mask_in[j * own + l]
                gb[l] += pb * mask_in[j * own + l]

        each(0, nz, one)

    def stage_gate():
        def one(k):
            r = pl.ds(pl.multiple_of(k * BLK, BLK), BLK)
            gf = gate[k].astype(F32)
            uf = up[k].astype(F32)
            s = jax.nn.sigmoid(gf)
            f1[r, :] = uf * s * (1.0 + gf * (1.0 - s))
            f2[r, :] = gf * s

        each(0, nblk, one)

    def stage_side():
        each(1, nz, lambda d: crossed(bb, bk_s, bk_r, d))

        def one(k):
            p = ab[slot_of[k]]
            t = tail_unpack(p[full * 64 :].astype(F32)).astype(BF16)
            first = jnp.concatenate([p[i * 64 : (i + 1) * 64] for i in range(full)] + [t], axis=1)
            back = tail_unpack(bb[owner_of[k]].astype(F32)).astype(BF16)
            r = pl.ds(pl.multiple_of(k * BLK, BLK), BLK)
            acc[r, :] += dot(back, first, 1, 0)

        each(0, nblk, one)

    tile = rows // 3

    def multiply(z, h, wref):
        for t in range(3):
            r = pl.ds(t * tile, tile)
            acc[r, :] += dot(ogb[2 * z + h, r, :], wref, 1, 1)

    def own_w():
        for h in (0, 1):
            multiply(g, h, w[:, h * d_loc : (h + 1) * d_loc])

    def multiply_step(s):
        def one(c):
            d, h = lax.div(c, 2), lax.rem(c, 2)
            z = lax.rem(g + jnp.where(d == 0, nz - s, s), nz)
            multiply(z, h, wb[z, h])

        each(0, 4, one)

    stages = [stage_partial, stage_sum, stage_back, stage_grads, stage_gate, stage_side]
    asteps = list(range(1, aring.size))
    done = [False]

    def relay_a():
        if asteps:
            s = asteps.pop(0)
            aring.relay(s, s == aring.size - 1)
        elif not done[0]:
            done[0] = True
            aring.finish()

    for s in range(1, wring.size):
        relay_a()
        wring.relay(s, s == wring.size - 1)
        relay_a()
        if s == 1:
            own_w()
        multiply_step(s)
        if len(stages) > 1 or (stages and done[0]):
            stages.pop(0)()
    while not done[0]:
        relay_a()
    for stage in stages:
        stage()
    wring.finish()

    def last(c):
        z = lax.rem(g + nz // 2, nz)
        multiply(z, c, wb[z, c])

    each(0, 2, last)

    def out(k):
        r = pl.ds(pl.multiple_of(k * BLK, BLK), BLK)
        x = acc[r, :]
        dg[r, :] = (x * f1[r, :]).astype(BF16)
        du[r, :] = (x * f2[r, :]).astype(BF16)

    each(0, nblk, out)

    plane.sent()
    wring.sent()
    aring.sent()
    each(1, nz, lambda d: cross(hs, hr, x_s, x_r, d).wait_send())
    each(1, mp, lambda d: flat(part, rsb, False, rs_s, rs_r, d).wait_send())
    each(1, mp, lambda d: flat(fac, fac, True, fg_s, fg_r, d).wait_send())
    each(1, nz, lambda d: cross(bs, bb, bk_s, bk_r, d).wait_send())


def shards(og, gate, up, w, a, b, aob, soa):
    nz, mp = lax.axis_size("dp"), lax.axis_size("mp")
    rows, d_loc = og.shape
    ff = gate.shape[1]
    own = a.shape[0]
    nblk = rows // BLK
    g = lax.axis_index("dp")
    match = aob[:, None] == jnp.arange(soa.shape[0], dtype=jnp.int32)[None, :]
    slot = jnp.sum(jnp.where(match, soa[None, :], 0), axis=1).reshape(nz, nblk)
    owner = slot // own
    mine = lax.dynamic_index_in_dim(owner, g, 0, keepdims=False)
    slot_of = lax.dynamic_index_in_dim(slot, g, 0, keepdims=False)
    to_owner = mine[None, :] == jnp.arange(nz, dtype=jnp.int32)[:, None]
    blk_of = jnp.sum(jnp.where(to_owner, jnp.arange(nblk, dtype=jnp.int32)[None, :], 0), axis=1)
    hit_of = jnp.sum(to_owner.astype(F32), axis=1)
    here = owner == g
    slot_in = jnp.sum(jnp.where(here, slot % own, 0), axis=1)
    is_slot = here[:, None, :] & (
        (slot % own)[:, None, :] == jnp.arange(own, dtype=jnp.int32)[None, :, None]
    )
    mask_in = jnp.sum(is_slot.astype(F32), axis=2).reshape(nz * own)
    packed = ff * 64 // 128
    send = (ff + d_loc) * 64 // 128
    vm = pl.BlockSpec(memory_space=pltpu.VMEM)
    sm = pl.BlockSpec(memory_space=pltpu.SMEM)
    dma = pltpu.SemaphoreType.DMA
    return pl.pallas_call(
        functools.partial(kernel, nz, mp),
        out_shape=(
            jax.ShapeDtypeStruct((rows, ff), BF16),
            jax.ShapeDtypeStruct((rows, ff), BF16),
            jax.ShapeDtypeStruct((own, RANK, ff), F32),
            jax.ShapeDtypeStruct((own, RANK, d_loc), F32),
        ),
        in_specs=[sm] * 6 + [vm] * 7,
        out_specs=(vm,) * 4,
        scratch_shapes=[
            pltpu.VMEM((mp, rows, d_loc), BF16),
            pltpu.VMEM((nz, 2, ff, d_loc), BF16),
            pltpu.VMEM((nz * own, packed, 128), BF16),
            pltpu.VMEM((nz, send, 128), BF16),
            pltpu.VMEM((nz, send, 128), BF16),
            pltpu.VMEM((mp, 32, 128), F32),
            pltpu.VMEM((mp, 32, 128), F32),
            pltpu.VMEM((mp, 32, 128), BF16),
            pltpu.VMEM((nz, 32, 128), BF16),
            pltpu.VMEM((nz, 32, 128), BF16),
            pltpu.VMEM((rows, ff), F32),
            pltpu.VMEM((rows, ff), F32),
            pltpu.VMEM((rows, ff), F32),
            dma((2, 2, mp // 2)), dma((2, 2, mp // 2)),
            dma((2, 2, nz // 2)), dma((2, 2, nz // 2)),
            dma((2, 2, nz // 2)), dma((2, 2, nz // 2)),
            dma((nz,)), dma((nz,)),
            dma((mp,)), dma((mp,)),
            dma((mp,)), dma((mp,)),
            dma((nz,)), dma((nz,)),
            dma((2,)),
        ],
        compiler_params=pltpu.CompilerParams(
            collective_id=0, has_side_effects=True, vmem_limit_bytes=60 * 1024 * 1024
        ),
    )(
        blk_of, slot_in, slot_of, mine, hit_of, mask_in, og, og.reshape(nblk, BLK, d_loc),
        gate.reshape(nblk, BLK, ff), up.reshape(nblk, BLK, ff), w, a, b,
    )


def solution(mesh):
    in_specs = (
        P("dp", "mp"),
        P("dp", "mp"),
        P("dp", "mp"),
        P("mp", "dp"),
        P("dp", None, "mp"),
        P("dp", None, "mp"),
        P(),
        P(),
    )
    out_specs = (P("dp", "mp"), P("dp", "mp"), P("dp", None, "mp"), P("dp", None, "mp"))
    return jax.shard_map(shards, mesh=mesh, in_specs=in_specs, out_specs=out_specs, check_vma=False)
```

time: 353 us -> 219 us (0.62)
  waiting for transfers between devices: 240 us -> 0 us
  Pallas kernels: 0 us -> 205 us
  starting transfers between devices: 49.8 us -> 0 us
  matrix products: 20.5 us -> 0 us
  between operations: 15.8 us -> 0.68 us
  other arithmetic: 10.5 us -> 2.04 us
  local copies, waits for them, and re-layouts: 16 us -> 10.9 us
    pallas_call x0 -> x1, Pallas kernels: none -> 205 us  [shards(): pl.pallas_call(functools.partial(kernel, nz, mp), out_shape=(jax.ShapeDty...]
    psum x1 -> x0, waiting for transfers between devices: 123 us -> none  [shards(): lax.psum(jnp.concatenate([down_part, back_part], axis=2), 'mp')]
    all_to_all x4 -> x0, waiting for transfers between devices: 94.7 us -> none  [the longest x1 67.1 us: in_one_piece(): lax.all_to_all(both, axis, split_axis=split_dim, concat_axis=concat_dim,...]
    all_to_all x4 -> x0, starting transfers between devices: 49.7 us -> none  [the longest x1 15.9 us: in_one_piece(): lax.all_to_all(both, axis, split_axis=split_dim, concat_axis=concat_dim,...]
    all_gather x2 -> x0, waiting for transfers between devices: 21.3 us -> none  [the longest x1 21.2 us: shards(): out_whole = lax.all_gather(output_gradient, 'mp', axis=1, tiled=True)]
    dot_general x8 -> x0, matrix products: 20.5 us -> none  [the longest x1 14.9 us: shards(): lax.dot_general(out_whole, lax.all_gather(down_weight, 'dp', axis=1, tile...]
    gather x7 -> x0, local copies, waits for them, and re-layouts: 6.47 us -> none  [the longest x1 1.82 us: shards(): jnp.take(a_recv.reshape(groups * capacity, ADAPTER_RANK, ff_local), own_i...]
    unnamed x18, local copies, waits for them, and re-layouts: 1.75 us -> 5.98 us
  transfers between devices with their start and end apart: 7 -> 0, of which waited for: 5 -> 0; matrix products, arithmetic and copies ran while one was open for 6% -> 0% of each run, Pallas kernels for 0% -> 0%
where the time goes in v1:
time: 219 us
  Pallas kernels  205 us (94%)
  local copies, waits for them, and re-layouts  10.9 us (5%)
    pallas_call x1, Pallas kernels, shards(): pl.pallas_call(functools.partial(kernel, nz, mp), out_shape=(jax.ShapeDty...  205 us
    unnamed x18, local copies, waits for them, and re-layouts  5.98 us

profile of v1, /device:TPU:1, one launch (start us, length us, event | category | flops | bytes accessed | tf_op | source)
XLA Modules:
  0.0 219.0 jit_solution(9875668399090038674)
XLA Ops:
  0.6 0.0 copy-start.5
  0.6 0.0 copy-start.6
  0.7 0.7 copy-done.5
  1.3 0.0 copy-done.6
  1.3 0.1 select_reduce_fusion
  1.4 0.1 reshape.75
  1.5 0.6 select_reduce_fusion.1
  2.1 0.5 dynamic-slice_bitcast_fusion
  2.7 0.0 copy-start.4
  2.7 0.6 convert_reduce_fusion.1.hit_of
  3.3 0.0 copy-done.4
  3.3 0.6 select_reduce_fusion.2.blk_of
  3.9 0.1 copy.20
  4.0 0.1 copy.21
  4.1 0.1 copy.22
  4.2 0.6 reshape.76.mask_in
  4.9 0.0 copy-start.1
  4.9 2.3 %copy.23 = bf16[768,448]{1,0:T(8,128)(2,1)} copy(bf16[768,448]{0,1:T(8,128)(2,1)} %param.9) | data formatting | bytes 1376256 | tf_op args[1]
  7.2 0.0 copy-done.1
  7.2 1.2 copy.24
  8.4 205.4 %shard_map.111 = (bf16[768,448]{1,0:T(8,128)(2,1)}, bf16[768,448]{1,0:T(8,128)(2,1)}, f32[4,64,448]{2,1,0:T(8,128)}, f32[4,64,256]{2,1,0:T(8,128)}) custom-call(s32[16]{0:T(128)} %select_reduce_fusion.2.blk_of, s32[16]{0:T(128)} %get-tuple-element.16.slot_in, s32[12]{0:T(128)} %get-tuple-element.20.slot_of, s32[12]{0:T(128)} %copy-done.4, ...), custom_call_target="tpu_custom_call" | custom-call | tf_op jit(solution)/shard_map/pallas_call | solution.py:395
  213.8 0.0 copy-start
  213.8 2.3 %copy.25 = bf16[768,448]{0,1:T(8,128)(2,1)} copy(bf16[768,448]{1,0:T(8,128)(2,1)} %get-tuple-element.12) | data formatting | bytes 1376256 | tf_op jit(solution)/shard_map/pallas_call | solution.py:395
  216.1 0.0 copy-done
  216.1 0.0 copy-start.2
  216.1 1.1 copy.26
  217.2 0.0 copy-done.2
  217.2 0.0 copy-start.3
  217.2 0.8 copy.29
  218.0 0.3 copy-done.3
  218.3 0.7 copy.30
  (1 shorter events, 0.0 us)
Async XLA Ops:
  0.6 0.7 copy-start.5
  0.6 0.7 copy-start.6
  2.7 0.7 copy-start.4
  4.9 2.3 %copy-start.1 = (bf16[768,448]{0,1:T(8,128)(2,1)S(1)}, bf16[768,448]{0,1:T(8,128)(2,1)}, u32[]{:S(2)}) copy-start(bf16[768,448]{0,1:T(8,128)(2,1)} %param.10) | copy-start | bytes 2064388
  213.8 2.3 %copy-start = (bf16[768,448]{1,0:T(8,128)(2,1)S(1)}, bf16[768,448]{1,0:T(8,128)(2,1)}, u32[]{:S(2)}) copy-start(bf16[768,448]{1,0:T(8,128)(2,1)} %get-tuple-element.13) | copy-start | bytes 2064388
  216.1 1.1 copy-start.2
  217.2 1.1 copy-start.3

commit v2 on v1

v2 whole, which is shorter than its diff:
```python
import functools
import math

import jax
import jax.numpy as jnp
from jax import lax
from jax.experimental import pallas as pl
from jax.experimental.pallas import tpu as pltpu
from jax.sharding import PartitionSpec as P

BLK = 64
RANK = 64
MESH = pl.DeviceIdType.MESH
F32 = jnp.float32
BF16 = jnp.bfloat16


def dot(x, y, cx, cy):
    return lax.dot_general(x, y, (((cx,), (cy,)), ((), ())), preferred_element_type=F32)


def each(lo, hi, body):
    def step(i, carry):
        body(i)
        return carry

    if hi > lo:
        lax.fori_loop(lo, hi, step, 0)


def same(x, y):
    return 1 - jnp.minimum(jnp.abs(x - y), 1)


def swap(x):
    return pltpu.roll(x, 64, 1)


def kernel(
    nz, mp,
    aob, soa, og, og3, gate, up, w, a, b,
    out, ga, gb,
    ogb, wb, ab, asel, apk, asend, og3v, gv, uv, av, bv, hp, hs, hr, xb, part, rsb, fac, bk1, bk2, gap,
    blk_of, hit_of, slot_in, mask_in, a_at, sel_at, sel_of, owner_of,
    og_s, og_r, w_s, w_r, a_s, a_r, x_s, x_r, rs_s, rs_r, fg_s, fg_r, bk_s, bk_r, bc_s, bc_r,
    sl_s, sl_r, xb_s, xb_r, loc, tok,
):
    xs = math.isqrt(mp // 2)
    ys = mp // 2 // xs
    rows, d_loc = og.shape
    ff = gate.shape[0]
    nblk = rows // BLK
    own = a.shape[0]
    half_rows = rows // 2
    fh = ff // 2
    units = nz * 8 // mp
    tail = min(3, nz // 2 - 1)
    reach = (nz // 2 - tail, nz // 2 - 1 - tail)
    quarter = nz // 4
    mid = (fh + d_loc // 2) // 2
    g = lax.axis_index("dp")
    m = lax.axis_index("mp")
    sign = 1 - 2 * lax.rem(m, 2)

    def ring_to_mp(q):
        p, c = lax.div(q, 2), lax.rem(q, 2)
        y = lax.div(p, xs)
        x = lax.rem(lax.rem(p, xs) + ys * xs - y, xs)
        return (y * xs + x) * 2 + c

    chip = lax.div(m, 2)
    row = lax.div(chip, xs)
    q = (xs * row + lax.rem(lax.rem(chip, xs) + row, xs)) * 2 + lax.rem(m, 2)

    def wrap(r):
        return lax.rem(r + 2 * nz, nz)

    def local(src, dst, k):
        return pltpu.make_async_copy(src, dst, loc.at[k])

    locals_ = [
        local(a, av, 0), local(gate, gv, 1), local(up, uv, 2), local(og3, og3v, 3),
        local(b, bv, 4), local(og, ogb.at[m], 5),
        local(w.at[:, pl.ds(0, d_loc)], wb.at[g, 0], 6),
        local(w.at[:, pl.ds(d_loc, d_loc)], wb.at[g, 1], 7),
    ]
    for c in locals_:
        c.start()

    bar = pltpu.get_barrier_semaphore()
    for d in (1, nz - 1):
        pl.semaphore_signal(bar, inc=1, device_id=(wrap(g + d), m), device_id_type=MESH)
    for d in (1, mp - 1):
        pl.semaphore_signal(
            bar, inc=1, device_id=(g, ring_to_mp(lax.rem(q + d, mp))), device_id_type=MESH
        )
    pl.semaphore_wait(bar, 4)

    known = nz // 2 - 1

    def token(d):
        pl.semaphore_signal(
            tok.at[d], inc=1, device_id=(wrap(g + (1 if d == 0 else -1)), m), device_id_type=MESH
        )

    def pass_tokens():
        for d in (0, 1):
            pl.semaphore_wait(tok.at[d], 1)
            token(d)

    class Ring:
        def __init__(self, n, pos, sign, counts, peer, first, buf, ssem, rsem):
            self.n, self.pos, self.sign, self.counts = n, pos, sign, counts
            self.peer, self.first, self.buf, self.ssem, self.rsem = peer, first, buf, ssem, rsem
            self.size = max(max(c) for c in counts)

        def at(self, d, s):
            step = self.sign * s if d == 0 else -self.sign * s
            return lax.rem(self.pos + 2 * self.n - step, self.n)

        def copy(self, d, h, s, src=None):
            dst = self.buf(self.at(d, s), h)
            return pltpu.make_async_remote_copy(
                src_ref=dst if src is None else src,
                dst_ref=dst,
                send_sem=self.ssem.at[d, h, s],
                recv_sem=self.rsem.at[d, h, s],
                device_id=self.peer(self.at(d, -1)),
                device_id_type=MESH,
            )

        def begin(self):
            for h in (0, 1):
                for d in (0, 1):
                    if self.counts[d][h] > 0:
                        self.copy(d, h, 0, self.first(h)).start()

        def arrived(self, d, h, s):
            ref = self.buf(self.at(d, s + 1), h)
            pltpu.make_async_remote_copy(
                src_ref=ref,
                dst_ref=ref,
                send_sem=self.ssem.at[d, h, s],
                recv_sem=self.rsem.at[d, h, s],
                device_id=self.peer(self.pos),
                device_id_type=MESH,
            ).wait_recv()

        def relay(self, s, k=None):
            k = s if k is None else k
            for h in (0, 1):
                for d in (0, 1):
                    if k - 1 < self.counts[d][h]:
                        self.arrived(d, h, s - 1)
                    if k < self.counts[d][h]:
                        self.copy(d, h, s).start()

        def sent(self):
            for h in (0, 1):
                for d in (0, 1):
                    each(
                        0, self.counts[d][h],
                        lambda s, d=d, h=h: self.copy(d, h, s).wait_send(),
                    )

    def halves(n):
        return ((n // 2, n // 2 - 1), (n // 2 - 1, n // 2))

    plane = Ring(
        mp, q, 1, halves(mp), lambda r: (g, ring_to_mp(r)),
        lambda h: og.at[pl.ds(h * half_rows, half_rows), :],
        lambda r, h: ogb.at[ring_to_mp(r), pl.ds(h * half_rows, half_rows), :],
        og_s, og_r,
    )
    wring = Ring(
        nz, g, 1, halves(nz), lambda r: (r, m),
        lambda h: w.at[:, pl.ds(h * d_loc, d_loc)],
        lambda r, h: wb.at[r, h],
        w_s, w_r,
    )

    def some_a(r, h):
        return ab.at[pl.ds(r * own + h * (own // 2), own // 2)]

    aring = Ring(
        nz, g, sign, tuple((r, r) for r in reach), lambda r: (r, m),
        lambda h: apk.at[pl.ds(h * (own // 2), own // 2)], some_a, a_s, a_r,
    )

    wring.begin()
    plane.begin()
    for d in (0, 1):
        token(d)

    lane = lax.broadcasted_iota(jnp.int32, (fh, 128), 1)
    lane64 = lax.broadcasted_iota(jnp.int32, (RANK, 128), 1)

    locals_[0].wait()
    eye = (
        lax.broadcasted_iota(jnp.int32, (RANK, 128), 0) == lane64
    ).astype(F32).astype(BF16)
    for l in range(own):
        t = dot(av[l], eye, 0, 0)
        t = jnp.where(lane < 64, t[:fh], swap(t[fh:])).astype(BF16)
        apk[l] = t
        ab[g * own + l] = t
    aring.begin()

    slots = [soa[aob[g * nblk + k]] for k in range(nblk)]
    owners = [lax.div(s, own) for s in slots]

    def block_for(o):
        at, hit = jnp.int32(0), jnp.int32(0)
        for k in range(nblk):
            e = same(owners[k], o)
            at, hit = at + k * e, hit + e
        blk_of[o] = jnp.minimum(at, nblk - 1)
        hit_of[o] = hit.astype(F32)

    each(0, nz, block_for)

    locals_[1].wait()
    locals_[2].wait()

    def tile_of(j):
        c = pl.ds(pl.multiple_of(j * 128, 128), 128)
        gf = gv[:, c].astype(F32)
        h = gf * jax.nn.sigmoid(gf) * uv[:, c].astype(F32)
        hp[2 * j] = jnp.where(lane < 64, h[:fh], swap(h[fh:])).astype(BF16)
        hp[2 * j + 1] = jnp.where(lane < 64, swap(h[:fh]), h[fh:]).astype(BF16)

    both = min(known - 1, nblk // 2)

    def tile_and_token(j):
        tile_of(j)
        pass_tokens()

    each(0, both, tile_and_token)
    each(both, nblk // 2, tile_of)
    locals_[3].wait()

    def fill(o):
        at, hit = blk_of[o], hit_of[o]
        hs[o, :fh] = (hp[at].astype(F32) * hit).astype(BF16)
        x = (og3v[at].astype(F32) * hit).astype(BF16)
        for k in range(d_loc // 128):
            hs[o, fh + k * 64 : fh + (k + 1) * 64] = x[:, k * 128 : (k + 1) * 128]

    each(0, nz, fill)
    each(both, known - 1, lambda j: pass_tokens())
    for d in (0, 1):
        pl.semaphore_wait(tok.at[d], 1)

    def remote(src, dst, ssem, rsem, z, p):
        return pltpu.make_async_remote_copy(
            src_ref=src, dst_ref=dst, send_sem=ssem, recv_sem=rsem,
            device_id=(z, p), device_id_type=MESH,
        )

    far = wrap(g + nz // 2)

    def piece(ref, i):
        return ref.at[pl.ds(i * mid, mid)]

    def leg1(i):
        to = wrap(g + (quarter if i == 0 else -quarter))
        return remote(piece(hs.at[far], i), xb.at[i], xb_s.at[0, i], xb_r.at[0, i], to, m)

    def leg2(i):
        d = quarter if i == 0 else -quarter
        dst = piece(hr.at[wrap(g - d)], i)
        return remote(xb.at[i], dst, xb_s.at[1, i], xb_r.at[1, i], wrap(g + d), m)

    def leg2_in(i):
        ref = piece(hr.at[far], i)
        return remote(ref, ref, xb_s.at[1, i], xb_r.at[1, i], g, m)

    def block_copy(d):
        to = wrap(g + d)
        return remote(hs.at[to], hr.at[g], x_s.at[d], x_r.at[d], to, m)

    def block_in(d):
        ref = hr.at[wrap(g - d)]
        remote(ref, ref, x_s.at[d], x_r.at[d], g, m).wait_recv()

    def others(body):
        each(1, nz // 2, body)
        each(nz // 2 + 1, nz, body)

    for i in (0, 1):
        leg1(i).start()
    others(lambda d: block_copy(d).start())
    own_hs = local(hs.at[g], hr.at[g], 8)
    own_hs.start()

    def group_tables(j):
        hit, at = jnp.int32(0), jnp.int32(0)
        for k in range(nblk):
            s = soa[aob[j * nblk + k]]
            e = same(lax.div(s, own), g)
            hit, at = hit + e, at + e * lax.rem(s, own)
        slot_in[j] = jnp.minimum(at, own - 1)
        for l in range(own):
            mask_in[j * own + l] = (hit * same(at, l)).astype(F32)

    each(0, nz, group_tables)
    for k in range(nblk):
        o = owners[k]
        dist = lax.rem(sign * (g - o) + nz, nz)
        picked = jnp.minimum(jnp.maximum(dist - reach[0], 0), 1) * jnp.minimum(
            jnp.maximum(nz - reach[1] - dist, 0), 1
        )
        a_at[k] = picked * (g * own) + (1 - picked) * slots[k]
        sel_at[k] = picked * o + (1 - picked) * wrap(g - sign * (reach[0] + 1))
        sel_of[k] = picked.astype(F32)
        owner_of[k] = o

    turn = min(6, plane.size - 1)
    each(1, turn, lambda s: plane.relay(s, 1))
    for i in (0, 1):
        remote(xb.at[i], xb.at[i], xb_s.at[0, i], xb_r.at[0, i], g, m).wait_recv()
        leg2(i).start()
    each(turn, plane.size - 1, lambda s: plane.relay(s, 1))
    plane.relay(plane.size - 1)
    plane.relay(plane.size)
    for c in locals_[4:]:
        c.wait()

    def grad_tile(j, k):
        return hr[j, fh + k * 64 : fh + (k + 1) * 64]

    def rows_of(ref, p):
        return ref.at[pl.ds(units * lax.div(p, 8), units), lax.rem(p, 8)]

    def part_copy(d):
        to = lax.rem(m + d, mp)
        return remote(rows_of(part, to), rsb.at[m], rs_s.at[d], rs_r.at[d], g, to)

    def part_in(d):
        ref = rsb.at[lax.rem(m + mp - d, mp)]
        remote(ref, ref, rs_s.at[d], rs_r.at[d], g, m).wait_recv()

    def fac_copy(d):
        to = lax.rem(m + d, mp)
        return remote(rows_of(fac, m), rows_of(fac, m), fg_s.at[d], fg_r.at[d], g, to)

    def fac_in(d):
        ref = rows_of(fac, lax.rem(m + mp - d, mp))
        remote(ref, ref, fg_s.at[d], fg_r.at[d], g, m).wait_recv()

    my_units = units * lax.div(m, 8)
    my_row = lax.rem(m, 8)

    def stage_partial():
        own_hs.wait()
        others(block_in)
        for i in (0, 1):
            leg2_in(i).wait_recv()

        def one(j):
            l = slot_in[j]
            z = dot(apk[l], hr[j, :fh], 0, 0)
            down = z[:64] + swap(z[64:])
            back = jnp.zeros((RANK, BLK), F32)
            for k in range(d_loc // 128):
                back += dot(bv[l, :, k * 128 : (k + 1) * 128], grad_tile(j, k), 1, 1)
            both = jnp.concatenate([down[:, :64], back], axis=1)
            part[j] = both.reshape(8, 8, 128)

        each(0, nz, one)
        each(1, mp, lambda d: part_copy(d).start())

    def stage_sum():
        rsb[m] = part[pl.ds(my_units, units), my_row]
        each(1, mp, part_in)
        total = lax.fori_loop(
            0, mp, lambda c, t: t + rsb[c], jnp.zeros((units, 8, 128), F32)
        )
        left = lax.broadcasted_iota(jnp.int32, (units, 8, 128), 2) < 64
        total = jnp.where(left, total, 2.0 * total).astype(BF16).astype(F32)
        fac[pl.ds(my_units, units), my_row] = total
        each(1, mp, lambda d: fac_copy(d).start())

    def back_copy(i):
        to = my_units + i
        return remote(fac.at[to, my_row], bk1.at[g], bk_s.at[i], bk_r.at[g], to, m)

    def back_in(o):
        remote(bk1.at[o], bk1.at[o], bk_s.at[0], bk_r.at[o], g, m).wait_recv()

    def stage_back():
        each(1, mp, fac_in)
        for i in range(units):
            @pl.when(my_units + i == g)
            def _():
                bk1[g] = fac[g, my_row]

            @pl.when(my_units + i != g)
            def _():
                back_copy(i).start()

    team = lax.div(g, units)

    def share_copy(d):
        to = lax.rem(m + d, mp)
        return remote(bk1, bk2.at[:, my_row], bc_s.at[d], bc_r.at[my_row], g, to)

    def stage_share():
        @pl.when(lax.div(m, 8) == team)
        def _():
            each(1, nz, lambda d: back_in(wrap(g + d)))
            each(1, mp, lambda d: share_copy(d).start())

    def stage_grads():
        gap[...] = jnp.zeros_like(gap)
        gb[...] = jnp.zeros_like(gb)

        def one(j):
            f = fac[j].reshape(RANK, 128)
            top = jnp.where(lane64 < 64, swap(f), 0.0).astype(BF16)
            bot = jnp.where(lane64 < 64, 0.0, f).astype(BF16)
            pa = dot(jnp.concatenate([top, bot], axis=0), hr[j, :fh], 1, 1)
            pa = pa.astype(BF16).astype(F32)
            down = f.astype(BF16)[:, :64]
            for k in range(d_loc // 128):
                c = slice(k * 128, (k + 1) * 128)
                pb = (2.0 * dot(down, grad_tile(j, k), 1, 0)).astype(BF16).astype(F32)
                for l in range(own):
                    gb[l, :, c] += pb * mask_in[j * own + l]
            for l in range(own):
                gap[l] += pa * mask_in[j * own + l]

        each(0, nz, one)
        for l in range(own):
            ga[l] = jnp.concatenate([gap[l, :64], gap[l, 64:]], axis=1)

    def picks():
        return ((0, wrap(g - sign * reach[0]), sign), (1, wrap(g + sign * reach[1]), -sign))

    def pick_copy(d, o, step, k):
        to = wrap(g + step * k)
        return remote(
            asend.at[d * 3 + k - 1], asel.at[o], sl_s.at[d, k - 1], sl_r.at[d, k - 1], to, m
        )

    def pick_send():
        for d, o, step in picks():
            for k in range(1, tail + 1):
                to = wrap(g + step * k)
                at = jnp.int32(0)
                for i in range(nblk):
                    s = soa[aob[to * nblk + i]]
                    at = at + same(lax.div(s, own), o) * lax.rem(s, own)
                asend[d * 3 + k - 1] = ab[o * own + jnp.minimum(at, own - 1)]
        for d, o, step in picks():
            for k in range(1, tail + 1):
                pick_copy(d, o, step, k).start()

    def pick_in():
        for k in range(1, tail + 1):
            for d, o in ((0, wrap(g - sign * (reach[0] + k))), (1, wrap(g + sign * (reach[1] + k)))):
                ref = asel.at[o]
                remote(ref, ref, sl_s.at[d, k - 1], sl_r.at[d, k - 1], g, m).wait_recv()

    def stage_side():
        pick_in()

        def row_in(t):
            ref = bk2.at[:, t]

            @pl.when(units_first + t != m)
            def _():
                remote(ref, ref, bc_s.at[0], bc_r.at[t], g, m).wait_recv()

        units_first = 8 * team

        @pl.when(lax.div(m, 8) == team)
        def _():
            bk2[:, my_row] = bk1[...]

        each(0, 8, row_in)

        def first_of(k):
            near, sel = ab[a_at[k]].astype(F32), asel[sel_at[k]].astype(F32)
            return near * (1.0 - sel_of[k]) + sel * sel_of[k]

        def one(j):
            a1, a2 = first_of(2 * j), first_of(2 * j + 1)
            top = jnp.where(lane < 64, a1, swap(a2)).astype(BF16)
            bot = jnp.where(lane < 64, swap(a1), a2).astype(BF16)
            b1 = bk2[owner_of[2 * j]].reshape(RANK, 128)
            b2 = bk2[owner_of[2 * j + 1]].reshape(RANK, 128)
            r = jnp.concatenate(
                [jnp.where(lane64 < 64, swap(b1), 0.0), jnp.where(lane64 < 64, 0.0, b2)], axis=0
            ).astype(BF16)
            c = pl.ds(pl.multiple_of(j * 128, 128), 128)
            out[:fh, c] += dot(top, r, 1, 0)
            out[fh:, c] += dot(bot, r, 1, 0)

        each(0, nblk // 2, one)

    tile = 256 if rows % 256 == 0 else 128

    def multiply(z, h, fresh=False):
        x = wb[z, h]
        for t in range(rows // tile):
            c = slice(t * tile, (t + 1) * tile)
            y = dot(x, ogb[2 * z + h, c, :], 1, 1)
            if fresh:
                out[:, c] = y
            else:
                out[:, c] += y

    def multiply_step(s):
        def one(c):
            d, h = lax.div(c, 2), lax.rem(c, 2)
            multiply(wrap(g + (2 * d - 1) * s), h)

        each(0, 4, one)

    stages = [stage_partial, stage_sum, stage_back, stage_share, stage_grads, stage_side]
    a_steps = [functools.partial(aring.relay, s) for s in range(1, reach[0] + 1)] + [pick_send]
    for s in range(1, nz // 2):
        if a_steps:
            a_steps.pop(0)()
        wring.relay(s)
        if a_steps:
            a_steps.pop(0)()
        if s == 1:
            multiply(g, 0, True)
            multiply(g, 1)
        multiply_step(s)
        if stages and (len(stages) > 1 or not a_steps):
            stages.pop(0)()
    for f in a_steps + stages:
        f()
    wring.relay(nz // 2)
    each(0, 2, lambda c: multiply(far, c))

    plane.sent()
    wring.sent()
    aring.sent()
    others(lambda d: block_copy(d).wait_send())
    for i in (0, 1):
        leg1(i).wait_send()
        leg2(i).wait_send()
    each(1, mp, lambda d: part_copy(d).wait_send())
    each(1, mp, lambda d: fac_copy(d).wait_send())
    for i in range(units):
        @pl.when(my_units + i != g)
        def _():
            back_copy(i).wait_send()

    @pl.when(lax.div(m, 8) == team)
    def _():
        each(1, mp, lambda d: share_copy(d).wait_send())

    for d, o, step in picks():
        for k in range(1, tail + 1):
            pick_copy(d, o, step, k).wait_send()


def shards(og, gate, up, w, a, b, aob, soa):
    nz, mp = lax.axis_size("dp"), lax.axis_size("mp")
    rows, d_loc = og.shape
    ff = gate.shape[1]
    own = a.shape[0]
    nblk = rows // BLK
    fh = ff // 2
    send = fh + d_loc // 2
    units = nz * 8 // mp
    gate, up = gate.T, up.T
    vm = pl.BlockSpec(memory_space=pltpu.VMEM)
    sm = pl.BlockSpec(memory_space=pltpu.SMEM)
    hbm = pl.BlockSpec(memory_space=pl.ANY)
    dma = pltpu.SemaphoreType.DMA
    d_hidden, ga, gb = pl.pallas_call(
        functools.partial(kernel, nz, mp),
        out_shape=(
            jax.ShapeDtypeStruct((ff, rows), F32),
            jax.ShapeDtypeStruct((own, RANK, ff), F32),
            jax.ShapeDtypeStruct((own, RANK, d_loc), F32),
        ),
        in_specs=[sm] * 2 + [hbm] * 7,
        out_specs=(vm,) * 3,
        scratch_shapes=[
            pltpu.VMEM((mp, rows, d_loc), BF16),
            pltpu.VMEM((nz, 2, ff, d_loc), BF16),
            pltpu.VMEM((nz * own, fh, 128), BF16),
            pltpu.VMEM((nz, fh, 128), BF16),
            pltpu.VMEM((own, fh, 128), BF16),
            pltpu.VMEM((6, fh, 128), BF16),
            pltpu.VMEM((nblk, BLK, d_loc), BF16),
            pltpu.VMEM((ff, rows), BF16),
            pltpu.VMEM((ff, rows), BF16),
            pltpu.VMEM((own, RANK, ff), BF16),
            pltpu.VMEM((own, RANK, d_loc), BF16),
            pltpu.VMEM((nblk, fh, 128), BF16),
            pltpu.VMEM((nz, send, 128), BF16),
            pltpu.VMEM((nz, send, 128), BF16),
            pltpu.VMEM((2, send // 2, 128), BF16),
            pltpu.VMEM((nz, 8, 8, 128), F32),
            pltpu.VMEM((mp, units, 8, 128), F32),
            pltpu.VMEM((nz, 8, 8, 128), F32),
            pltpu.VMEM((nz, 8, 128), F32),
            pltpu.VMEM((nz, 8, 8, 128), F32),
            pltpu.VMEM((own, 2 * RANK, fh), F32),
            pltpu.SMEM((nz,), jnp.int32),
            pltpu.SMEM((nz,), F32),
            pltpu.SMEM((nz,), jnp.int32),
            pltpu.SMEM((nz * own,), F32),
            pltpu.SMEM((nblk,), jnp.int32),
            pltpu.SMEM((nblk,), jnp.int32),
            pltpu.SMEM((nblk,), F32),
            pltpu.SMEM((nblk,), jnp.int32),
            dma((2, 2, mp // 2)), dma((2, 2, mp // 2)),
            dma((2, 2, nz // 2)), dma((2, 2, nz // 2)),
            dma((2, 2, nz // 2)), dma((2, 2, nz // 2)),
            dma((nz,)), dma((nz,)),
            dma((mp,)), dma((mp,)),
            dma((mp,)), dma((mp,)),
            dma((units,)), dma((nz,)),
            dma((mp,)), dma((8,)),
            dma((2, 3)), dma((2, 3)),
            dma((2, 2)), dma((2, 2)),
            dma((9,)),
            pltpu.SemaphoreType.REGULAR((2,)),
        ],
        compiler_params=pltpu.CompilerParams(
            collective_id=0, has_side_effects=True, vmem_limit_bytes=48 * 1024 * 1024
        ),
    )(aob, soa, og, og.reshape(nblk, BLK, d_loc), gate, up, w, a, b)
    gf, uf = gate.astype(F32), up.astype(F32)
    s = jax.nn.sigmoid(gf)
    d_gate = (d_hidden * uf * s * (1.0 + gf * (1.0 - s))).astype(BF16)
    d_up = (d_hidden * (gf * s)).astype(BF16)
    return d_gate.T, d_up.T, ga, gb


def solution(mesh):
    in_specs = (
        P("dp", "mp"),
        P("dp", "mp"),
        P("dp", "mp"),
        P("mp", "dp"),
        P("dp", None, "mp"),
        P("dp", None, "mp"),
        P(),
        P(),
    )
    out_specs = (P("dp", "mp"), P("dp", "mp"), P("dp", None, "mp"), P("dp", None, "mp"))
    return jax.shard_map(shards, mesh=mesh, in_specs=in_specs, out_specs=out_specs, check_vma=False)
```

time: 219 us -> 231 us (1.055)
  Pallas kernels: 205 us -> 219 us
    pallas_call x1, Pallas kernels: 205 us -> 219 us  [shards(): pl.pallas_call(functools.partial(kernel, nz, mp), out_shape=(jax.ShapeDty...]
    pallas_call x2 -> x0, local copies, waits for them, and re-layouts: 3.42 us -> none  [shards(): pl.pallas_call(functools.partial(kernel, nz, mp), out_shape=(jax.ShapeDty...]
    unnamed x18, local copies, waits for them, and re-layouts: 5.98 us -> 8.88 us
where the time goes in v2:
time: 231 us; the launch traced here: 230 us
  Pallas kernels  219 us (95%)
  local copies, waits for them, and re-layouts  8.88 us (4%)
    pallas_call x1, Pallas kernels, shards(): pl.pallas_call(functools.partial(kernel, nz, mp), out_shape=(jax.ShapeDty...  219 us
    unnamed x18, local copies, waits for them, and re-layouts  8.88 us

profile of v2, /device:TPU:1, one launch (start us, length us, event | category | flops | bytes accessed | tf_op | source)
XLA Modules:
  0.0 230.4 jit_solution(2872170206793200741)
XLA Ops:
  0.6 0.0 copy-start
  0.6 1.1 copy-done
  1.7 0.0 copy-start.1
  1.7 1.1 copy-done.1
  2.8 0.0 copy-start.2
  2.8 1.0 copy-done.2
  3.8 0.0 copy-start.3
  3.8 1.0 copy-done.3
  4.8 0.0 copy-start.4
  4.9 0.9 copy-done.4
  5.8 0.0 copy-start.5
  5.8 0.9 copy-done.5
  6.7 0.0 copy-start.6
  6.7 0.7 copy-done.6
  7.4 0.0 copy-start.7
  7.4 0.7 copy-done.7
  8.0 219.1 %shard_map.111 = (f32[448,768]{1,0:T(8,128)S(1)}, f32[4,64,448]{2,1,0:T(8,128)S(1)}, f32[4,64,256]{2,1,0:T(8,128)S(1)}) custom-call(s32[192]{0:T(256)S(1)} %copy-done.6, s32[64]{0:T(128)S(1)} %copy-done.7, bf16[768,256]{1,0:T(8,128)(2,1)S(1)} %copy-done.2, bf16[12,64,256]{2,1,0:T(8,128)(2,1)S(1)} %bitcast.12, bf16[448,768]{1,0:T(8,128)(2,1)S(1)} %bitcast.10, ...), custom_call_target="tpu_custom_call" | custom-call | tf_op jit(solution)/shard_map/pallas_call | solution.py:577
  227.1 1.8 fusion.8
  228.9 0.8 copy.14
  229.7 0.7 copy.15
Async XLA Ops:
  0.6 1.1 copy-start
  1.7 1.1 copy-start.1
  2.8 1.0 copy-start.2
  3.8 1.0 copy-start.3
  4.8 0.9 copy-start.4
  5.8 0.9 copy-start.5
  6.7 0.7 copy-start.6
  7.4 0.7 copy-start.7

commit v3 on v2

--- a/solution.py
+++ b/solution.py
@@ -40,8 +40,8 @@
     nz, mp,
     aob, soa, og, og3, gate, up, w, a, b,
     out, ga, gb,
-    ogb, wb, ab, asel, apk, asend, og3v, gv, uv, av, bv, hp, hs, hr, xb, part, rsb, fac, bk1, bk2, gap,
-    blk_of, hit_of, slot_in, mask_in, a_at, sel_at, sel_of, owner_of,
+    ogb, wb, ab, asel, apk, asend, og3v, gv, uv, av, bv, hp, hs, hr, xb, part, rsb, fac, bk1, shs, bk2, gap,
+    blk_of, hit_of, slot_in, mask_in, a_at, sel_at, sel_of, quad_of, half_of, odd_of,
     og_s, og_r, w_s, w_r, a_s, a_r, x_s, x_r, rs_s, rs_r, fg_s, fg_r, bk_s, bk_r, bc_s, bc_r,
     sl_s, sl_r, xb_s, xb_r, loc, tok,
 ):
@@ -313,14 +313,11 @@
         a_at[k] = picked * (g * own) + (1 - picked) * slots[k]
         sel_at[k] = picked * o + (1 - picked) * wrap(g - sign * (reach[0] + 1))
         sel_of[k] = picked.astype(F32)
-        owner_of[k] = o
-
-    turn = min(6, plane.size - 1)
-    each(1, turn, lambda s: plane.relay(s, 1))
-    for i in (0, 1):
-        remote(xb.at[i], xb.at[i], xb_s.at[0, i], xb_r.at[0, i], g, m).wait_recv()
-        leg2(i).start()
-    each(turn, plane.size - 1, lambda s: plane.relay(s, 1))
+        quad_of[k] = lax.div(o, 4)
+        half_of[k] = lax.rem(lax.div(o, 2), 2).astype(F32)
+        odd_of[k] = lax.rem(o, 2).astype(F32)
+
+    each(1, plane.size - 1, lambda s: plane.relay(s, 1))
     plane.relay(plane.size - 1)
     plane.relay(plane.size)
     for c in locals_[4:]:
@@ -403,12 +400,20 @@
 
     def share_copy(d):
         to = lax.rem(m + d, mp)
-        return remote(bk1, bk2.at[:, my_row], bc_s.at[d], bc_r.at[my_row], g, to)
+        return remote(shs, bk2.at[:, my_row], bc_s.at[d], bc_r.at[my_row], g, to)
 
     def stage_share():
         @pl.when(lax.div(m, 8) == team)
         def _():
             each(1, nz, lambda d: back_in(wrap(g + d)))
+            for i in range(nz // 4):
+                pairs = [
+                    jnp.where(lane64[:8] < 64, swap(bk1[4 * i + 2 * h]), bk1[4 * i + 2 * h + 1])
+                    for h in (0, 1)
+                ]
+                x = jnp.concatenate(pairs, axis=0).astype(BF16)
+                shs[i] = x
+                bk2[i, my_row] = x
             each(1, mp, lambda d: share_copy(d).start())
 
     def stage_grads():
@@ -474,24 +479,29 @@
 
         units_first = 8 * team
 
-        @pl.when(lax.div(m, 8) == team)
-        def _():
-            bk2[:, my_row] = bk1[...]
-
         each(0, 8, row_in)
 
         def first_of(k):
             near, sel = ab[a_at[k]].astype(F32), asel[sel_at[k]].astype(F32)
             return near * (1.0 - sel_of[k]) + sel * sel_of[k]
+
+        def back_of(k, side):
+            x = bk2[quad_of[k]].astype(F32)
+            x = x[:, :8] * (1.0 - half_of[k]) + x[:, 8:] * half_of[k]
+            x = x.reshape(RANK, 128)
+            keep = odd_of[k] if side else 1.0 - odd_of[k]
+            return x * keep + swap(x) * (1.0 - keep)
 
         def one(j):
             a1, a2 = first_of(2 * j), first_of(2 * j + 1)
             top = jnp.where(lane < 64, a1, swap(a2)).astype(BF16)
             bot = jnp.where(lane < 64, swap(a1), a2).astype(BF16)
-            b1 = bk2[owner_of[2 * j]].reshape(RANK, 128)
-            b2 = bk2[owner_of[2 * j + 1]].reshape(RANK, 128)
             r = jnp.concatenate(
-                [jnp.where(lane64 < 64, swap(b1), 0.0), jnp.where(lane64 < 64, 0.0, b2)], axis=0
+                [
+                    jnp.where(lane64 < 64, back_of(2 * j, 0), 0.0),
+                    jnp.where(lane64 < 64, 0.0, back_of(2 * j + 1, 1)),
+                ],
+                axis=0,
             ).astype(BF16)
             c = pl.ds(pl.multiple_of(j * 128, 128), 128)
             out[:fh, c] += dot(top, r, 1, 0)
@@ -518,7 +528,12 @@
 
         each(0, 4, one)
 
-    stages = [stage_partial, stage_sum, stage_back, stage_share, stage_grads, stage_side]
+    def stage_legs():
+        for i in (0, 1):
+            remote(xb.at[i], xb.at[i], xb_s.at[0, i], xb_r.at[0, i], g, m).wait_recv()
+            leg2(i).start()
+
+    stages = [stage_legs, stage_partial, stage_sum, stage_back, stage_share, stage_grads, stage_side]
     a_steps = [functools.partial(aring.relay, s) for s in range(1, reach[0] + 1)] + [pick_send]
     for s in range(1, nz // 2):
         if a_steps:
@@ -603,7 +618,8 @@
             pltpu.VMEM((mp, units, 8, 128), F32),
             pltpu.VMEM((nz, 8, 8, 128), F32),
             pltpu.VMEM((nz, 8, 128), F32),
-            pltpu.VMEM((nz, 8, 8, 128), F32),
+            pltpu.VMEM((nz // 4, 16, 128), BF16),
+            pltpu.VMEM((nz // 4, 8, 16, 128), BF16),
             pltpu.VMEM((own, 2 * RANK, fh), F32),
             pltpu.SMEM((nz,), jnp.int32),
             pltpu.SMEM((nz,), F32),
@@ -613,6 +629,8 @@
             pltpu.SMEM((nblk,), jnp.int32),
             pltpu.SMEM((nblk,), F32),
             pltpu.SMEM((nblk,), jnp.int32),
+            pltpu.SMEM((nblk,), F32),
+            pltpu.SMEM((nblk,), F32),
             dma((2, 2, mp // 2)), dma((2, 2, mp // 2)),
             dma((2, 2, nz // 2)), dma((2, 2, nz // 2)),
             dma((2, 2, nz // 2)), dma((2, 2, nz // 2)),
@@ -627,7 +645,7 @@
             pltpu.SemaphoreType.REGULAR((2,)),
         ],
         compiler_params=pltpu.CompilerParams(
-            collective_id=0, has_side_effects=True, vmem_limit_bytes=48 * 1024 * 1024
+            collective_id=0, has_side_effects=True, vmem_limit_bytes=67_000_000
         ),
     )(aob, soa, og, og.reshape(nblk, BLK, d_loc), gate, up, w, a, b)
     gf, uf = gate.astype(F32), up.astype(F32)

time: 231 us -> 199 us (0.86)
  Pallas kernels: 219 us -> 194 us
  local copies, waits for them, and re-layouts: 8.88 us -> 1.5 us
    pallas_call x1, Pallas kernels: 219 us -> 194 us  [shards(): pl.pallas_call(functools.partial(kernel, nz, mp), out_shape=(jax.ShapeDty...]
    unnamed x18 -> x6, local copies, waits for them, and re-layouts: 8.88 us -> 1.5 us
where the time goes in v3:
time: 199 us
  Pallas kernels  194 us (97%)
  other arithmetic  3.53 us (2%)
    pallas_call x1, Pallas kernels, shards(): pl.pallas_call(functools.partial(kernel, nz, mp), out_shape=(jax.ShapeDty...  194 us

profile of v3, /device:TPU:1, one launch (start us, length us, event | category | flops | bytes accessed | tf_op | source)
XLA Modules:
  0.0 199.2 jit_solution(13813291680367560907)
XLA Ops:
  0.6 193.5 %shard_map.111 = (f32[448,768]{1,0:T(8,128)}, f32[4,64,448]{2,1,0:T(8,128)}, f32[4,64,256]{2,1,0:T(8,128)}) custom-call(s32[192]{0:T(256)} %aob.1, s32[64]{0:T(128)} %soa.1, bf16[768,256]{1,0:T(8,128)(2,1)} %og.1, bf16[12,64,256]{2,1,0:T(8,128)(2,1)} %bitcast.12, bf16[448,768]{1,0:T(8,128)(2,1)} %bitcast.10, bf16[448,768]{1,0:T(8,128)(2,1)} %bitcast.11, ...), custom_call_target="tpu_custom_call" | custom-call | tf_op jit(solution)/shard_map/pallas_call | solution.py:592
  194.2 0.0 copy-start
  194.2 0.0 copy-start.1
  194.2 3.5 %fusion.8 = (bf16[768,448]{0,1:T(8,128)(2,1)}, bf16[768,448]{0,1:T(8,128)(2,1)}) fusion(f32[448,768]{1,0:T(8,128)} %get-tuple-element.7, bf16[768,448]{0,1:T(8,128)(2,1)} %param.9, bf16[768,448]{0,1:T(8,128)(2,1)} %param.10), kind=kLoop, calls=%fused_computation.11 | loop fusion | flops 5160960 | bytes 4128768 | tf_op jit(solution)/shard_map/transpose | solution.py:655
  197.7 0.0 copy-done
  197.7 0.8 copy.14
  198.5 0.0 copy-done.1
  198.5 0.7 copy.15
Async XLA Ops:
  194.2 3.6 %copy-start = (f32[4,64,448]{2,1,0:T(8,128)S(1)}, f32[4,64,448]{2,1,0:T(8,128)}, u32[]{:S(2)}) copy-start(f32[4,64,448]{2,1,0:T(8,128)} %get-tuple-element.18) | copy-start | bytes 1376260
  194.2 4.3 %copy-start.1 = (f32[4,64,256]{2,1,0:T(8,128)S(1)}, f32[4,64,256]{2,1,0:T(8,128)}, u32[]{:S(2)}) copy-start(f32[4,64,256]{2,1,0:T(8,128)} %get-tuple-element.19) | copy-start | bytes 786436

commit v4 on v3

--- a/solution.py
+++ b/solution.py
@@ -317,7 +317,10 @@
         half_of[k] = lax.rem(lax.div(o, 2), 2).astype(F32)
         odd_of[k] = lax.rem(o, 2).astype(F32)
 
-    each(1, plane.size - 1, lambda s: plane.relay(s, 1))
+    cut = plane.size // 2
+    each(1, cut, lambda s: plane.relay(s, 1))
+    wring.relay(1)
+    each(cut, plane.size - 1, lambda s: plane.relay(s, 1))
     plane.relay(plane.size - 1)
     plane.relay(plane.size)
     for c in locals_[4:]:
@@ -538,9 +541,8 @@
     for s in range(1, nz // 2):
         if a_steps:
             a_steps.pop(0)()
-        wring.relay(s)
-        if a_steps:
-            a_steps.pop(0)()
+        if s > 1:
+            wring.relay(s)
         if s == 1:
             multiply(g, 0, True)
             multiply(g, 1)

time: 199 us -> 196 us (0.985); the launches traced: 199 us -> 192 us
  Pallas kernels: 194 us -> 186 us
    pallas_call x1, Pallas kernels: 194 us -> 186 us  [shards(): pl.pallas_call(functools.partial(kernel, nz, mp), out_shape=(jax.ShapeDty...]
where the time goes in v4:
time: 196 us; the launch traced here: 192 us
  Pallas kernels  186 us (95%)
  other arithmetic  3.53 us (2%)
    pallas_call x1, Pallas kernels, shards(): pl.pallas_call(functools.partial(kernel, nz, mp), out_shape=(jax.ShapeDty...  186 us

profile of v4, /device:TPU:1, one launch (start us, length us, event | category | flops | bytes accessed | tf_op | source)
XLA Modules:
  0.0 192.0 jit_solution(15764150467732920021)
XLA Ops:
  0.6 186.3 %shard_map.111 = (f32[448,768]{1,0:T(8,128)}, f32[4,64,448]{2,1,0:T(8,128)}, f32[4,64,256]{2,1,0:T(8,128)}) custom-call(s32[192]{0:T(256)} %aob.1, s32[64]{0:T(128)} %soa.1, bf16[768,256]{1,0:T(8,128)(2,1)} %og.1, bf16[12,64,256]{2,1,0:T(8,128)(2,1)} %bitcast.12, bf16[448,768]{1,0:T(8,128)(2,1)} %bitcast.10, bf16[448,768]{1,0:T(8,128)(2,1)} %bitcast.11, ...), custom_call_target="tpu_custom_call" | custom-call | tf_op jit(solution)/shard_map/pallas_call | solution.py:594
  186.9 0.0 copy-start
  186.9 0.0 copy-start.1
  186.9 3.5 %fusion.8 = (bf16[768,448]{0,1:T(8,128)(2,1)}, bf16[768,448]{0,1:T(8,128)(2,1)}) fusion(f32[448,768]{1,0:T(8,128)} %get-tuple-element.7, bf16[768,448]{0,1:T(8,128)(2,1)} %param.9, bf16[768,448]{0,1:T(8,128)(2,1)} %param.10), kind=kLoop, calls=%fused_computation.11 | loop fusion | flops 5160960 | bytes 4128768 | tf_op jit(solution)/shard_map/transpose | solution.py:657
  190.5 0.0 copy-done
  190.5 0.8 copy.14
  191.3 0.0 copy-done.1
  191.3 0.7 copy.15
Async XLA Ops:
  186.9 3.6 %copy-start = (f32[4,64,448]{2,1,0:T(8,128)S(1)}, f32[4,64,448]{2,1,0:T(8,128)}, u32[]{:S(2)}) copy-start(f32[4,64,448]{2,1,0:T(8,128)} %get-tuple-element.18) | copy-start | bytes 1376260
  186.9 4.3 %copy-start.1 = (f32[4,64,256]{2,1,0:T(8,128)S(1)}, f32[4,64,256]{2,1,0:T(8,128)}, u32[]{:S(2)}) copy-start(f32[4,64,256]{2,1,0:T(8,128)} %get-tuple-element.19) | copy-start | bytes 786436

commit v5 on v4

--- a/solution.py
+++ b/solution.py
@@ -39,8 +39,8 @@
 def kernel(
     nz, mp,
     aob, soa, og, og3, gate, up, w, a, b,
-    out, ga, gb,
-    ogb, wb, ab, asel, apk, asend, og3v, gv, uv, av, bv, hp, hs, hr, xb, part, rsb, fac, bk1, shs, bk2, gap,
+    out, ga_out, gb_out,
+    ogb, wb, ab, asel, apk, asend, og3v, gv, uv, av, bv, hp, hs, hr, xb, part, rsb, fac, bk1, shs, bk2, gap, ga, gb,
     blk_of, hit_of, slot_in, mask_in, a_at, sel_at, sel_of, quad_of, half_of, odd_of,
     og_s, og_r, w_s, w_r, a_s, a_r, x_s, x_r, rs_s, rs_r, fg_s, fg_r, bk_s, bk_r, bc_s, bc_r,
     sl_s, sl_r, xb_s, xb_r, loc, tok,
@@ -441,6 +441,8 @@
         each(0, nz, one)
         for l in range(own):
             ga[l] = jnp.concatenate([gap[l, :64], gap[l, 64:]], axis=1)
+        local(ga, ga_out, 9).start()
+        local(gb, gb_out, 10).start()
 
     def picks():
         return ((0, wrap(g - sign * reach[0]), sign), (1, wrap(g + sign * reach[1]), -sign))
@@ -554,6 +556,8 @@
     wring.relay(nz // 2)
     each(0, 2, lambda c: multiply(far, c))
 
+    local(ga, ga_out, 9).wait()
+    local(gb, gb_out, 10).wait()
     plane.sent()
     wring.sent()
     aring.sent()
@@ -599,7 +603,7 @@
             jax.ShapeDtypeStruct((own, RANK, d_loc), F32),
         ),
         in_specs=[sm] * 2 + [hbm] * 7,
-        out_specs=(vm,) * 3,
+        out_specs=(vm, hbm, hbm),
         scratch_shapes=[
             pltpu.VMEM((mp, rows, d_loc), BF16),
             pltpu.VMEM((nz, 2, ff, d_loc), BF16),
@@ -623,6 +627,8 @@
             pltpu.VMEM((nz // 4, 16, 128), BF16),
             pltpu.VMEM((nz // 4, 8, 16, 128), BF16),
             pltpu.VMEM((own, 2 * RANK, fh), F32),
+            pltpu.VMEM((own, RANK, ff), F32),
+            pltpu.VMEM((own, RANK, d_loc), F32),
             pltpu.SMEM((nz,), jnp.int32),
             pltpu.SMEM((nz,), F32),
             pltpu.SMEM((nz,), jnp.int32),
@@ -643,7 +649,7 @@
             dma((mp,)), dma((8,)),
             dma((2, 3)), dma((2, 3)),
             dma((2, 2)), dma((2, 2)),
-            dma((9,)),
+            dma((11,)),
             pltpu.SemaphoreType.REGULAR((2,)),
         ],
         compiler_params=pltpu.CompilerParams(

time: 196 us -> 195 us (level)
  no operation moved by 1% of the time
where the time goes in v5:
time: 195 us; the launch traced here: 192 us
  Pallas kernels  186 us (95%)
  other arithmetic  3.53 us (2%)
    pallas_call x1, Pallas kernels, shards(): pl.pallas_call(functools.partial(kernel, nz, mp), out_shape=(jax.ShapeDty...  186 us

profile of v5, /device:TPU:1, one launch (start us, length us, event | category | flops | bytes accessed | tf_op | source)
XLA Modules:
  0.0 191.7 jit_solution(6992413304733312893)
XLA Ops:
  0.6 186.0 %shard_map.111 = (f32[448,768]{1,0:T(8,128)}, f32[4,64,448]{2,1,0:T(8,128)}, f32[4,64,256]{2,1,0:T(8,128)}) custom-call(s32[192]{0:T(256)} %aob.1, s32[64]{0:T(128)} %soa.1, bf16[768,256]{1,0:T(8,128)(2,1)} %og.1, bf16[12,64,256]{2,1,0:T(8,128)(2,1)} %bitcast.12, bf16[448,768]{1,0:T(8,128)(2,1)} %bitcast.10, bf16[448,768]{1,0:T(8,128)(2,1)} %bitcast.11, ...), custom_call_target="tpu_custom_call" | custom-call | tf_op jit(solution)/shard_map/pallas_call | solution.py:598
  186.7 0.0 copy-start
  186.7 0.0 copy-start.1
  186.7 3.5 %fusion.8 = (bf16[768,448]{0,1:T(8,128)(2,1)}, bf16[768,448]{0,1:T(8,128)(2,1)}) fusion(f32[448,768]{1,0:T(8,128)} %get-tuple-element.7, bf16[768,448]{0,1:T(8,128)(2,1)} %param.9, bf16[768,448]{0,1:T(8,128)(2,1)} %param.10), kind=kLoop, calls=%fused_computation.11 | loop fusion | flops 5160960 | bytes 4128768 | tf_op jit(solution)/shard_map/transpose | solution.py:663
  190.2 0.0 copy-done
  190.2 0.8 copy.14
  191.0 0.0 copy-done.1
  191.0 0.7 copy.15
Async XLA Ops:
  186.7 3.6 %copy-start = (f32[4,64,448]{2,1,0:T(8,128)S(1)}, f32[4,64,448]{2,1,0:T(8,128)}, u32[]{:S(2)}) copy-start(f32[4,64,448]{2,1,0:T(8,128)} %get-tuple-element.18) | copy-start | bytes 1376260
  186.7 4.3 %copy-start.1 = (f32[4,64,256]{2,1,0:T(8,128)S(1)}, f32[4,64,256]{2,1,0:T(8,128)}, u32[]{:S(2)}) copy-start(f32[4,64,256]{2,1,0:T(8,128)} %get-tuple-element.19) | copy-start | bytes 786436
